TPU v7x, 128 devices: a whole 4x4x4 slice. The times are simulated.
128 devices in a mesh: patch: 16 (over y, x), col: 8 (over z, core).
Axes of the slice: x: 4, y: 4, z: 4, core: 2. Of those that a mesh axis runs over, the one named last changes fastest.
Arguments:
- potential0: float32 [512, 16, 128], P(('patch', 'col')), may hold values from -3 to 3
- source_term: float32 [512, 16, 128], P(('patch', 'col')), may hold values from -9 to 9
- self_coef: float32 [512, 128], P(('patch', 'col')), may hold values from 1 to 4
- nearfield: float32 [512, 24, 128, 128], P(('patch', 'col')), may hold values from -0.109375 to 0.109375
- precond: float32 [512, 128, 128], P(('patch', 'col')), may hold values from -1 to 2
- exch_current: float32 [512, 128], P(('patch', 'col')), may hold values from 0.05 to 0.5
- conductance: float32 [512, 128], P(('patch', 'col')), may hold values from 0.1 to 1
- member: int32 [512, 128], P(('patch', 'col')), may hold values from 0 to 63
- anode_drive: float32 [64], replicated, may hold values from -1 to 1
- pair_source: int32 [512, 24], P(('patch', 'col')), may hold values from 0 to 39
- pair_count: int32 [512], P(('patch', 'col')), may hold values from 1 to 24, as said below
Outputs:
- potential: float32 [512, 16, 128], P(('patch', 'col'))
- residual: float32 [512, 16, 128], P(('patch', 'col'))
Inputs may be any that keep to these rules, and one draw needn't show every extreme that they name: Slots k < pair_count[b] of block b are live; some block has all 24 slots live, and the blocks of some devices hold far more live pairs than those of others.
All inputs are finite; a program needn't handle non-finite values.
Results may differ from a plain program's by a relative error of at most 0.0003.
Values sent between devices are 32-bit elements; how exact they have to be, the bound alone decides.
A program may use at most 64 MiB of HBM per device.

v0:
```python
import jax
import jax.numpy as jnp
from jax import lax
from jax.sharding import PartitionSpec as P

NEWTON = 2
GMRES = 2
ALPHA = 0.6
BETA = 0.4
EPS = 1e-06


def from_behind(array, axis, by):
    size = lax.axis_size(axis)
    return lax.ppermute(array, axis, [(i, (i + by) % size) for i in range(size)])


def column_sum(left, right):
    return jnp.sum(left * right, axis=(0, 2))


def least_squares(columns, beta):
    depth = len(columns)
    hessen = jnp.zeros((beta.shape[0], depth + 1, depth), jnp.float32)
    for place in range(depth):
        hessen = hessen.at[:, : place + 2, place].set(columns[place].T)
    gram = jnp.einsum("cij,cik->cjk", hessen, hessen, precision=lax.Precision.HIGHEST)
    right = beta[:, None] * hessen[:, 0, :]
    lower = jnp.linalg.cholesky(gram)
    middle = jax.scipy.linalg.solve_triangular(lower, right[:, :, None], lower=True)
    return jax.scipy.linalg.solve_triangular(lower, middle, lower=True, trans=1)[:, :, 0]


def body(
    potential0,
    source_term,
    self_coef,
    nearfield,
    precond,
    exch_current,
    conductance,
    member,
    anode_drive,
    pair_source,
    pair_count,
):
    pair_slots = pair_source.shape[1]
    live_mask = (jnp.arange(pair_slots, dtype=jnp.int32)[None, :] < pair_count[:, None]).astype(
        jnp.float32
    )
    members = anode_drive.shape[0]
    onehot = (jnp.arange(members, dtype=jnp.int32)[:, None, None] == member[None]).astype(
        jnp.float32
    )
    member_drive = jnp.sum(onehot * anode_drive[:, None, None], axis=0)
    diagonal = self_coef[:, None, :]
    current = exch_current[:, None, :]
    conduct = conductance[:, None, :]

    def near_field(field):
        own_patch = lax.all_gather(field, "col", axis=0, tiled=True)
        before = from_behind(field, "patch", 1)
        following = from_behind(field, "patch", -1)
        stacked = jnp.concatenate([own_patch, before, following], axis=0)
        sources = stacked[pair_source]
        return jnp.einsum(
            "bkij,bkcj->bci",
            nearfield,
            sources * live_mask[:, :, None, None],
            precision=lax.Precision.HIGHEST,
        )

    def mismatch(field, near_value):
        grow = jnp.exp(ALPHA * field)
        shrink = jnp.exp(-BETA * field)
        value = (
            diagonal * field
            + near_value
            + current * (grow - shrink)
            + conduct * (field - member_drive[:, None, :])
            - source_term
        )
        slope = current * (ALPHA * grow + BETA * shrink) + conduct
        return (value, slope)

    field = potential0
    near_now = near_field(field)
    for newton in range(NEWTON):
        value, slope = mismatch(field, near_now)
        start = -value
        beta = jnp.sqrt(lax.psum(column_sum(start, start), ("patch", "col")) + EPS)
        basis = [start / beta[None, :, None]]
        directions = []
        near_images = []
        columns = []
        for step in range(GMRES):
            direction = jnp.einsum(
                "bij,bcj->bci", precond, basis[step], precision=lax.Precision.HIGHEST
            )
            directions.append(direction)
            near_image = near_field(direction)
            near_images.append(near_image)
            image = diagonal * direction + near_image + slope * direction
            coeffs = []
            for place in range(step + 1):
                coeff = lax.psum(column_sum(basis[place], image), ("patch", "col"))
                image = image - coeff[None, :, None] * basis[place]
                coeffs.append(coeff)
            norm = jnp.sqrt(lax.psum(column_sum(image, image), ("patch", "col")) + EPS)
            basis.append(image / norm[None, :, None])
            columns.append(jnp.stack(coeffs + [norm]))
        weights = least_squares(columns, beta)
        update = jnp.zeros_like(field)
        for step in range(GMRES):
            update = update + weights[:, step][None, :, None] * directions[step]
        field = field + update
        near_now = near_field(field)
    final_value, final_slope = mismatch(field, near_now)
    return (field, final_value)


def solution(mesh):
    return jax.shard_map(
        body,
        mesh=mesh,
        in_specs=(
            P(("patch", "col"), None, None),
            P(("patch", "col"), None, None),
            P(("patch", "col"), None),
            P(("patch", "col"), None, None, None),
            P(("patch", "col"), None, None),
            P(("patch", "col"), None),
            P(("patch", "col"), None),
            P(("patch", "col"), None),
            P(),
            P(("patch", "col"), None),
            P(("patch", "col")),
        ),
        out_specs=(P(("patch", "col"), None, None), P(("patch", "col"), None, None)),
        check_vma=False,
    )
```

profile of v0, /device:TPU:1, one launch (start us, length us, event | category | flops | bytes accessed | tf_op | source)
XLA Modules:
  0.0 974.0 jit_solution(4111155873102971596)
XLA Ops:
  6.6 15.1 %all_gather.21 = f32[32,16,128]{2,1,0:T(8,128)S(1)} all-gather(f32[4,16,128]{2,1,0:T(8,128)} %param.24), channel_id=1, replica_groups=mesh['patch'=16,'col'=8] {'col'}, dimensions={0}, use_global_device_ids=true | all-gather | bytes 294912 | tf_op jit(solution)/shard_map/all_gather | solution.py:61
  24.7 7.6 multiply_reduce_fusion.11
  32.3 64.2 %psum.84 = f32[16]{0:T(128)S(1)} all-reduce(f32[16]{0:T(128)S(1)} %get-tuple-element.61), channel_id=1, replica_groups=mesh['patch'=16,'col'=8] {'patch','col'}, use_global_device_ids=true, to_apply=%region_2.0 | all-reduce | flops 16 | bytes 128 | tf_op jit(solution)/shard_map/psum | solution.py:91
  101.9 13.9 %all_gather.22 = f32[32,16,128]{2,1,0:T(8,128)S(1)} all-gather(f32[4,16,128]{2,1,0:T(8,128)S(1)} %fusion.43), channel_id=1, replica_groups=mesh['patch'=16,'col'=8] {'col'}, dimensions={0}, use_global_device_ids=true | all-gather | bytes 294912 | tf_op jit(solution)/shard_map/all_gather | solution.py:61
  116.5 7.5 multiply_reduce_fusion.10
  124.0 63.4 %psum.85 = f32[16]{0:T(128)S(1)} all-reduce(f32[16]{0:T(128)S(1)} %get-tuple-element.63), channel_id=1, replica_groups=mesh['patch'=16,'col'=8] {'patch','col'}, use_global_device_ids=true, to_apply=%region_4.0 | all-reduce | flops 16 | bytes 128 | tf_op jit(solution)/shard_map/psum | solution.py:106
  187.6 63.0 %psum.86 = f32[16]{0:T(128)S(1)} all-reduce(f32[16]{0:T(128)S(1)} %multiply_reduce_fusion.9), channel_id=1, replica_groups=mesh['patch'=16,'col'=8] {'patch','col'}, use_global_device_ids=true, to_apply=%region_6.0 | all-reduce | flops 16 | bytes 128 | tf_op jit(solution)/shard_map/psum | solution.py:109
  256.0 13.8 %all_gather.23 = f32[32,16,128]{2,1,0:T(8,128)S(1)} all-gather(f32[4,16,128]{2,1,0:T(8,128)S(1)} %fusion.44), channel_id=1, replica_groups=mesh['patch'=16,'col'=8] {'col'}, dimensions={0}, use_global_device_ids=true | all-gather | bytes 294912 | tf_op jit(solution)/shard_map/all_gather | solution.py:61
  270.5 7.5 multiply_reduce_fusion.8
  278.0 64.4 %psum.87 = f32[16]{0:T(128)S(1)} all-reduce(f32[16]{0:T(128)S(1)} %get-tuple-element.65), channel_id=1, replica_groups=mesh['patch'=16,'col'=8] {'patch','col'}, use_global_device_ids=true, to_apply=%region_8.0 | all-reduce | flops 16 | bytes 128 | tf_op jit(solution)/shard_map/psum | solution.py:106
  342.6 62.5 %psum.88 = f32[16]{0:T(128)S(1)} all-reduce(f32[16]{0:T(128)S(1)} %multiply_reduce_fusion.7), channel_id=1, replica_groups=mesh['patch'=16,'col'=8] {'patch','col'}, use_global_device_ids=true, to_apply=%region_10.0 | all-reduce | flops 16 | bytes 128 | tf_op jit(solution)/shard_map/psum | solution.py:106
  405.3 64.0 %psum.89 = f32[16]{0:T(128)S(1)} all-reduce(f32[16]{0:T(128)S(1)} %multiply_reduce_fusion.6), channel_id=1, replica_groups=mesh['patch'=16,'col'=8] {'patch','col'}, use_global_device_ids=true, to_apply=%region_12.0 | all-reduce | flops 16 | bytes 128 | tf_op jit(solution)/shard_map/psum | solution.py:109
  481.5 14.5 %all_gather.24 = f32[32,16,128]{2,1,0:T(8,128)S(1)} all-gather(f32[4,16,128]{2,1,0:T(8,128)S(1)} %add_add_fusion.1), channel_id=1, replica_groups=mesh['patch'=16,'col'=8] {'col'}, dimensions={0}, use_global_device_ids=true | all-gather | bytes 294912 | tf_op jit(solution)/shard_map/all_gather | solution.py:61
  496.7 7.5 multiply_reduce_fusion.5
  504.2 61.8 %psum.90 = f32[16]{0:T(128)S(1)} all-reduce(f32[16]{0:T(128)S(1)} %get-tuple-element.67), channel_id=1, replica_groups=mesh['patch'=16,'col'=8] {'patch','col'}, use_global_device_ids=true, to_apply=%region_16.0 | all-reduce | flops 16 | bytes 128 | tf_op jit(solution)/shard_map/psum | solution.py:91
  571.4 13.9 %all_gather.25 = f32[32,16,128]{2,1,0:T(8,128)S(1)} all-gather(f32[4,16,128]{2,1,0:T(8,128)S(1)} %fusion.45), channel_id=1, replica_groups=mesh['patch'=16,'col'=8] {'col'}, dimensions={0}, use_global_device_ids=true | all-gather | bytes 294912 | tf_op jit(solution)/shard_map/all_gather | solution.py:61
  593.5 63.5 %psum.91 = f32[16]{0:T(128)S(1)} all-reduce(f32[16]{0:T(128)S(1)} %get-tuple-element.69), channel_id=1, replica_groups=mesh['patch'=16,'col'=8] {'patch','col'}, use_global_device_ids=true, to_apply=%region_18.0 | all-reduce | flops 16 | bytes 128 | tf_op jit(solution)/shard_map/psum | solution.py:106
  657.1 62.6 %psum.92 = f32[16]{0:T(128)S(1)} all-reduce(f32[16]{0:T(128)S(1)} %multiply_reduce_fusion.3), channel_id=1, replica_groups=mesh['patch'=16,'col'=8] {'patch','col'}, use_global_device_ids=true, to_apply=%region_20.0 | all-reduce | flops 16 | bytes 128 | tf_op jit(solution)/shard_map/psum | solution.py:109
  725.0 14.0 %all_gather.26 = f32[32,16,128]{2,1,0:T(8,128)S(1)} all-gather(f32[4,16,128]{2,1,0:T(8,128)S(1)} %fusion.46), channel_id=1, replica_groups=mesh['patch'=16,'col'=8] {'col'}, dimensions={0}, use_global_device_ids=true | all-gather | bytes 294912 | tf_op jit(solution)/shard_map/all_gather | solution.py:61
  747.2 64.4 %psum.93 = f32[16]{0:T(128)S(1)} all-reduce(f32[16]{0:T(128)S(1)} %get-tuple-element.71), channel_id=1, replica_groups=mesh['patch'=16,'col'=8] {'patch','col'}, use_global_device_ids=true, to_apply=%region_22.0 | all-reduce | flops 16 | bytes 128 | tf_op jit(solution)/shard_map/psum | solution.py:106
  811.8 62.5 %psum.94 = f32[16]{0:T(128)S(1)} all-reduce(f32[16]{0:T(128)S(1)} %multiply_reduce_fusion.1), channel_id=1, replica_groups=mesh['patch'=16,'col'=8] {'patch','col'}, use_global_device_ids=true, to_apply=%region_24.0 | all-reduce | flops 16 | bytes 128 | tf_op jit(solution)/shard_map/psum | solution.py:106
  874.5 64.0 %psum.95 = f32[16]{0:T(128)S(1)} all-reduce(f32[16]{0:T(128)S(1)} %multiply_reduce_fusion), channel_id=1, replica_groups=mesh['patch'=16,'col'=8] {'patch','col'}, use_global_device_ids=true, to_apply=%region_26.0 | all-reduce | flops 16 | bytes 128 | tf_op jit(solution)/shard_map/psum | solution.py:109
  950.8 14.3 %all_gather.27 = f32[32,16,128]{2,1,0:T(8,128)S(1)} all-gather(f32[4,16,128]{2,1,0:T(8,128)S(1)} %add_add_fusion), channel_id=1, replica_groups=mesh['patch'=16,'col'=8] {'col'}, dimensions={0}, use_global_device_ids=true | all-gather | bytes 294912 | tf_op jit(solution)/shard_map/all_gather | solution.py:61
  965.8 8.0 fusion.3
  (123 shorter events, 75.1 us)
Async XLA Ops:
  0.6 95.9 %copy-start = (f32[4,128,128]{2,1,0:T(8,128)S(1)}, f32[4,128,128]{2,1,0:T(8,128)}, u32[]{:S(2)}) copy-start(f32[4,128,128]{2,1,0:T(8,128)} %param.28) | copy-start | bytes 786436
  0.6 115.9 %copy-start.1 = (f32[4,16,128]{2,1,0:T(8,128)S(1)}, f32[4,16,128]{2,1,0:T(8,128)}, u32[]{:S(2)}) copy-start(f32[4,16,128]{2,1,0:T(8,128)} %param.24) | copy-start | bytes 98308
  0.7 115.9 %copy-start.6 = (f32[4,128]{1,0:T(4,128)S(1)}, f32[4,128]{1,0:T(4,128)}, u32[]{:S(2)}) copy-start(f32[4,128]{1,0:T(4,128)} %param.26) | copy-start | bytes 6148
  0.7 115.9 %copy-start.5 = (f32[4,128]{1,0:T(4,128)S(1)}, f32[4,128]{1,0:T(4,128)}, u32[]{:S(2)}) copy-start(f32[4,128]{1,0:T(4,128)} %param.29) | copy-start | bytes 6148
  0.7 115.9 %copy-start.4 = (f32[4,128]{1,0:T(4,128)S(1)}, f32[4,128]{1,0:T(4,128)}, u32[]{:S(2)}) copy-start(f32[4,128]{1,0:T(4,128)} %param.30) | copy-start | bytes 6148
  0.7 23.3 %collective-permute-start = (f32[4,16,128]{2,1,0:T(8,128)}, f32[4,16,128]{2,1,0:T(8,128)S(1)}, u32[]{:S(2)}, u32[]{:S(2)}) collective-permute-start(f32[4,16,128]{2,1,0:T(8,128)} %param.24), channel_id=1, source_target_pairs={{0,8},{8,16},{16,24},{24,32},{32,40},{40,48},{48,56},{56,64},{64,7... | collective-permute-start | bytes 98312 | tf_op jit(solution)/shard_map/ppermute | solution.py:15
  2.8 21.2 %collective-permute-start.1 = (f32[4,16,128]{2,1,0:T(8,128)}, f32[4,16,128]{2,1,0:T(8,128)S(1)}, u32[]{:S(2)}, u32[]{:S(2)}) collective-permute-start(f32[4,16,128]{2,1,0:T(8,128)} %param.24), channel_id=1, source_target_pairs={{0,120},{8,0},{16,8},{24,16},{32,24},{40,32},{48,40},{56,48},{64,5... | collective-permute-start | bytes 98312 | tf_op jit(solution)/shard_map/ppermute | solution.py:15
  97.1 18.7 %collective-permute-start.2 = (f32[4,16,128]{2,1,0:T(8,128)S(1)}, f32[4,16,128]{2,1,0:T(8,128)S(1)}, u32[]{:S(2)}, u32[]{:S(2)}) collective-permute-start(f32[4,16,128]{2,1,0:T(8,128)S(1)} %fusion.43), channel_id=1, source_target_pairs={{0,8},{8,16},{16,24},{24,32},{32,40},{40,48},{48,56},{56,64},{64,7... | collective-permute-start | bytes 98312 | tf_op jit(solution)/shard_map/ppermute | solution.py:15
  97.3 18.4 %collective-permute-start.3 = (f32[4,16,128]{2,1,0:T(8,128)S(1)}, f32[4,16,128]{2,1,0:T(8,128)S(1)}, u32[]{:S(2)}, u32[]{:S(2)}) collective-permute-start(f32[4,16,128]{2,1,0:T(8,128)S(1)} %fusion.43), channel_id=1, source_target_pairs={{0,120},{8,0},{16,8},{24,16},{32,24},{40,32},{48,40},{56,48},{64,5... | collective-permute-start | bytes 98312 | tf_op jit(solution)/shard_map/ppermute | solution.py:15
  251.2 18.6 %collective-permute-start.4 = (f32[4,16,128]{2,1,0:T(8,128)S(1)}, f32[4,16,128]{2,1,0:T(8,128)S(1)}, u32[]{:S(2)}, u32[]{:S(2)}) collective-permute-start(f32[4,16,128]{2,1,0:T(8,128)S(1)} %fusion.44), channel_id=1, source_target_pairs={{0,8},{8,16},{16,24},{24,32},{32,40},{40,48},{48,56},{56,64},{64,7... | collective-permute-start | bytes 98312 | tf_op jit(solution)/shard_map/ppermute | solution.py:15
  252.1 17.7 %collective-permute-start.5 = (f32[4,16,128]{2,1,0:T(8,128)S(1)}, f32[4,16,128]{2,1,0:T(8,128)S(1)}, u32[]{:S(2)}, u32[]{:S(2)}) collective-permute-start(f32[4,16,128]{2,1,0:T(8,128)S(1)} %fusion.44), channel_id=1, source_target_pairs={{0,120},{8,0},{16,8},{24,16},{32,24},{40,32},{48,40},{56,48},{64,5... | collective-permute-start | bytes 98312 | tf_op jit(solution)/shard_map/ppermute | solution.py:15
  269.8 226.9 %copy-start.2 = (f32[4,16,128]{2,1,0:T(8,128)S(1)}, f32[4,16,128]{2,1,0:T(8,128)}, u32[]{:S(2)}) copy-start(f32[4,16,128]{2,1,0:T(8,128)} %param.25) | copy-start | bytes 98308
  476.7 19.3 %collective-permute-start.6 = (f32[4,16,128]{2,1,0:T(8,128)S(1)}, f32[4,16,128]{2,1,0:T(8,128)S(1)}, u32[]{:S(2)}, u32[]{:S(2)}) collective-permute-start(f32[4,16,128]{2,1,0:T(8,128)S(1)} %add_add_fusion.1), channel_id=1, source_target_pairs={{0,8},{8,16},{16,24},{24,32},{32,40},{40,48},{48,56},{56,64},{64,7... | collective-permute-start | bytes 98312 | tf_op jit(solution)/shard_map/ppermute | solution.py:15
  476.7 19.3 %collective-permute-start.7 = (f32[4,16,128]{2,1,0:T(8,128)S(1)}, f32[4,16,128]{2,1,0:T(8,128)S(1)}, u32[]{:S(2)}, u32[]{:S(2)}) collective-permute-start(f32[4,16,128]{2,1,0:T(8,128)S(1)} %add_add_fusion.1), channel_id=1, source_target_pairs={{0,120},{8,0},{16,8},{24,16},{32,24},{40,32},{48,40},{56,48},{64,5... | collective-permute-start | bytes 98312 | tf_op jit(solution)/shard_map/ppermute | solution.py:15
  566.6 18.7 %collective-permute-start.8 = (f32[4,16,128]{2,1,0:T(8,128)S(1)}, f32[4,16,128]{2,1,0:T(8,128)S(1)}, u32[]{:S(2)}, u32[]{:S(2)}) collective-permute-start(f32[4,16,128]{2,1,0:T(8,128)S(1)} %fusion.45), channel_id=1, source_target_pairs={{0,8},{8,16},{16,24},{24,32},{32,40},{40,48},{48,56},{56,64},{64,7... | collective-permute-start | bytes 98312 | tf_op jit(solution)/shard_map/ppermute | solution.py:15
  567.7 17.5 %collective-permute-start.9 = (f32[4,16,128]{2,1,0:T(8,128)S(1)}, f32[4,16,128]{2,1,0:T(8,128)S(1)}, u32[]{:S(2)}, u32[]{:S(2)}) collective-permute-start(f32[4,16,128]{2,1,0:T(8,128)S(1)} %fusion.45), channel_id=1, source_target_pairs={{0,120},{8,0},{16,8},{24,16},{32,24},{40,32},{48,40},{56,48},{64,5... | collective-permute-start | bytes 98312 | tf_op jit(solution)/shard_map/ppermute | solution.py:15
  720.2 18.8 %collective-permute-start.10 = (f32[4,16,128]{2,1,0:T(8,128)S(1)}, f32[4,16,128]{2,1,0:T(8,128)S(1)}, u32[]{:S(2)}, u32[]{:S(2)}) collective-permute-start(f32[4,16,128]{2,1,0:T(8,128)S(1)} %fusion.46), channel_id=1, source_target_pairs={{0,8},{8,16},{16,24},{24,32},{32,40},{40,48},{48,56},{56,64},{64,7... | collective-permute-start | bytes 98312 | tf_op jit(solution)/shard_map/ppermute | solution.py:15
  721.1 17.9 %collective-permute-start.11 = (f32[4,16,128]{2,1,0:T(8,128)S(1)}, f32[4,16,128]{2,1,0:T(8,128)S(1)}, u32[]{:S(2)}, u32[]{:S(2)}) collective-permute-start(f32[4,16,128]{2,1,0:T(8,128)S(1)} %fusion.46), channel_id=1, source_target_pairs={{0,120},{8,0},{16,8},{24,16},{32,24},{40,32},{48,40},{56,48},{64,5... | collective-permute-start | bytes 98312 | tf_op jit(solution)/shard_map/ppermute | solution.py:15
  945.9 27.9 %copy-start.3 = (f32[4,16,128]{2,1,0:T(8,128)}, f32[4,16,128]{2,1,0:T(8,128)S(1)}, u32[]{:S(2)}) copy-start(f32[4,16,128]{2,1,0:T(8,128)S(1)} %add_add_fusion) | copy-start | bytes 98308
  945.9 19.2 %collective-permute-start.12 = (f32[4,16,128]{2,1,0:T(8,128)S(1)}, f32[4,16,128]{2,1,0:T(8,128)S(1)}, u32[]{:S(2)}, u32[]{:S(2)}) collective-permute-start(f32[4,16,128]{2,1,0:T(8,128)S(1)} %add_add_fusion), channel_id=1, source_target_pairs={{0,8},{8,16},{16,24},{24,32},{32,40},{40,48},{48,56},{56,64},{64,7... | collective-permute-start | bytes 98312 | tf_op jit(solution)/shard_map/ppermute | solution.py:15
  946.0 19.1 %collective-permute-start.13 = (f32[4,16,128]{2,1,0:T(8,128)S(1)}, f32[4,16,128]{2,1,0:T(8,128)S(1)}, u32[]{:S(2)}, u32[]{:S(2)}) collective-permute-start(f32[4,16,128]{2,1,0:T(8,128)S(1)} %add_add_fusion), channel_id=1, source_target_pairs={{0,120},{8,0},{16,8},{24,16},{32,24},{40,32},{48,40},{56,48},{64,5... | collective-permute-start | bytes 98312 | tf_op jit(solution)/shard_map/ppermute | solution.py:15
where the time goes:
time: 984 us; the launch traced here: 974 us
  blocking collectives  860 us (87%)
  matrix products  55.7 us (6%)
  starting transfers between devices  34.8 us (4%)
  other arithmetic  16.5 us (2%)
    psum x6, blocking collectives, body(): coeff = lax.psum(column_sum(basis[place], image), ('patch', 'col'))  381 us
    psum x4, blocking collectives, body(): norm = jnp.sqrt(lax.psum(column_sum(image, image), ('patch', 'col')) + EPS)  254 us
    psum x2, blocking collectives, body(): beta = jnp.sqrt(lax.psum(column_sum(start, start), ('patch', 'col')) + EPS)  126 us
    all_gather x7, blocking collectives, near_field(): own_patch = lax.all_gather(field, 'col', axis=0, tiled=True)  99.4 us
    dot_general x7, matrix products, near_field(): jnp.einsum('bkij,bkcj->bci', nearfield, sources * live_mask[:, :, None, N...  52.9 us
    ppermute x14, starting transfers between devices, from_behind(): lax.ppermute(array, axis, [(i, (i + by) % size) for i in range(size)])  34.8 us
  transfers between devices with their start and end apart: 14, of which 0 were waited for; matrix products, arithmetic and copies ran while one was open for 0% of the time, Pallas kernels for 0%

commit v1 on v0

--- a/solution.py
+++ b/solution.py
@@ -88,7 +88,7 @@
     for newton in range(NEWTON):
         value, slope = mismatch(field, near_now)
         start = -value
-        beta = jnp.sqrt(lax.psum(column_sum(start, start), ("patch", "col")) + EPS)
+        beta = jnp.sqrt(lax.psum(lax.psum(column_sum(start, start), "col"), "patch") + EPS)
         basis = [start / beta[None, :, None]]
         directions = []
         near_images = []

time: 984 us -> 953 us (0.968)
  blocking collectives: 860 us -> 829 us
    psum x2 -> x4, blocking collectives: 126 us -> 82.5 us  [the longest x2 58.6 us: body(): lax.psum(lax.psum(column_sum(start, start), 'col'), 'patch') + EPS]
    all_gather x7, blocking collectives: 99.4 us -> 117 us  [near_field(): own_patch = lax.all_gather(field, 'col', axis=0, tiled=True)]
where the time goes in v1:
time: 953 us; the launch traced here: 943 us
  blocking collectives  829 us (87%)
  matrix products  55.7 us (6%)
  starting transfers between devices  34.9 us (4%)
  other arithmetic  16.5 us (2%)
    psum x6, blocking collectives, body(): coeff = lax.psum(column_sum(basis[place], image), ('patch', 'col'))  374 us
    psum x4, blocking collectives, body(): norm = jnp.sqrt(lax.psum(column_sum(image, image), ('patch', 'col')) + EPS)  255 us
    all_gather x7, blocking collectives, near_field(): own_patch = lax.all_gather(field, 'col', axis=0, tiled=True)  117 us
    psum x2, blocking collectives, body(): lax.psum(lax.psum(column_sum(start, start), 'col'), 'patch') + EPS  58.6 us
    dot_general x7, matrix products, near_field(): jnp.einsum('bkij,bkcj->bci', nearfield, sources * live_mask[:, :, None, N...  52.9 us
    ppermute x14, starting transfers between devices, from_behind(): lax.ppermute(array, axis, [(i, (i + by) % size) for i in range(size)])  34.9 us
    psum x2, blocking collectives, body(): lax.psum(column_sum(start, start), 'col')  23.9 us
  transfers between devices with their start and end apart: 14, of which 0 were waited for; matrix products, arithmetic and copies ran while one was open for 0% of the time, Pallas kernels for 0%

profile of v1, /device:TPU:1, one launch (start us, length us, event | category | flops | bytes accessed | tf_op | source)
XLA Modules:
  0.0 943.2 jit_solution(5481530788613409336)
XLA Ops:
  6.6 15.1 %all_gather.21 = f32[32,16,128]{2,1,0:T(8,128)S(1)} all-gather(f32[4,16,128]{2,1,0:T(8,128)} %param.24), channel_id=1, replica_groups=mesh['patch'=16,'col'=8] {'col'}, dimensions={0}, use_global_device_ids=true | all-gather | bytes 294912 | tf_op jit(solution)/shard_map/all_gather | solution.py:61
  24.7 7.6 multiply_reduce_fusion.11
  32.3 11.9 %psum.98 = f32[16]{0:T(128)S(1)} all-reduce(f32[16]{0:T(128)S(1)} %get-tuple-element.61), channel_id=1, replica_groups=mesh['patch'=16,'col'=8] {'col'}, use_global_device_ids=true, to_apply=%region_2.0 | all-reduce | flops 16 | bytes 128 | tf_op jit(solution)/shard_map/psum | solution.py:91
  44.2 30.1 %psum.99 = f32[16]{0:T(128)S(1)} all-reduce(f32[16]{0:T(128)S(1)} %psum.98), channel_id=1, replica_groups=mesh['patch'=16,'col'=8] {'patch'}, use_global_device_ids=true, to_apply=%region_3.0 | all-reduce | flops 16 | bytes 128 | tf_op jit(solution)/shard_map/psum | solution.py:91
  79.7 23.9 %all_gather.22 = f32[32,16,128]{2,1,0:T(8,128)S(1)} all-gather(f32[4,16,128]{2,1,0:T(8,128)S(1)} %fusion.43), channel_id=1, replica_groups=mesh['patch'=16,'col'=8] {'col'}, dimensions={0}, use_global_device_ids=true | all-gather | bytes 294912 | tf_op jit(solution)/shard_map/all_gather | solution.py:61
  111.8 61.8 %psum.100 = f32[16]{0:T(128)S(1)} all-reduce(f32[16]{0:T(128)S(1)} %get-tuple-element.63), channel_id=1, replica_groups=mesh['patch'=16,'col'=8] {'patch','col'}, use_global_device_ids=true, to_apply=%region_5.0 | all-reduce | flops 16 | bytes 128 | tf_op jit(solution)/shard_map/psum | solution.py:106
  173.8 63.5 %psum.101 = f32[16]{0:T(128)S(1)} all-reduce(f32[16]{0:T(128)S(1)} %multiply_reduce_fusion.9), channel_id=1, replica_groups=mesh['patch'=16,'col'=8] {'patch','col'}, use_global_device_ids=true, to_apply=%region_7.0 | all-reduce | flops 16 | bytes 128 | tf_op jit(solution)/shard_map/psum | solution.py:109
  242.7 14.6 %all_gather.23 = f32[32,16,128]{2,1,0:T(8,128)S(1)} all-gather(f32[4,16,128]{2,1,0:T(8,128)S(1)} %fusion.44), channel_id=1, replica_groups=mesh['patch'=16,'col'=8] {'col'}, dimensions={0}, use_global_device_ids=true | all-gather | bytes 294912 | tf_op jit(solution)/shard_map/all_gather | solution.py:61
  265.5 62.4 %psum.102 = f32[16]{0:T(128)S(1)} all-reduce(f32[16]{0:T(128)S(1)} %get-tuple-element.65), channel_id=1, replica_groups=mesh['patch'=16,'col'=8] {'patch','col'}, use_global_device_ids=true, to_apply=%region_9.0 | all-reduce | flops 16 | bytes 128 | tf_op jit(solution)/shard_map/psum | solution.py:106
  328.1 62.9 %psum.103 = f32[16]{0:T(128)S(1)} all-reduce(f32[16]{0:T(128)S(1)} %multiply_reduce_fusion.7), channel_id=1, replica_groups=mesh['patch'=16,'col'=8] {'patch','col'}, use_global_device_ids=true, to_apply=%region_11.0 | all-reduce | flops 16 | bytes 128 | tf_op jit(solution)/shard_map/psum | solution.py:106
  391.2 63.8 %psum.104 = f32[16]{0:T(128)S(1)} all-reduce(f32[16]{0:T(128)S(1)} %multiply_reduce_fusion.6), channel_id=1, replica_groups=mesh['patch'=16,'col'=8] {'patch','col'}, use_global_device_ids=true, to_apply=%region_13.0 | all-reduce | flops 16 | bytes 128 | tf_op jit(solution)/shard_map/psum | solution.py:109
  467.1 14.1 %all_gather.24 = f32[32,16,128]{2,1,0:T(8,128)S(1)} all-gather(f32[4,16,128]{2,1,0:T(8,128)S(1)} %add_add_fusion.1), channel_id=1, replica_groups=mesh['patch'=16,'col'=8] {'col'}, dimensions={0}, use_global_device_ids=true | all-gather | bytes 294912 | tf_op jit(solution)/shard_map/all_gather | solution.py:61
  482.0 7.5 multiply_reduce_fusion.5
  489.5 11.9 %psum.105 = f32[16]{0:T(128)S(1)} all-reduce(f32[16]{0:T(128)S(1)} %get-tuple-element.67), channel_id=1, replica_groups=mesh['patch'=16,'col'=8] {'col'}, use_global_device_ids=true, to_apply=%region_17.0 | all-reduce | flops 16 | bytes 128 | tf_op jit(solution)/shard_map/psum | solution.py:91
  501.4 28.5 %psum.106 = f32[16]{0:T(128)S(1)} all-reduce(f32[16]{0:T(128)S(1)} %psum.105), channel_id=1, replica_groups=mesh['patch'=16,'col'=8] {'patch'}, use_global_device_ids=true, to_apply=%region_18.0 | all-reduce | flops 16 | bytes 128 | tf_op jit(solution)/shard_map/psum | solution.py:91
  535.4 21.4 %all_gather.25 = f32[32,16,128]{2,1,0:T(8,128)S(1)} all-gather(f32[4,16,128]{2,1,0:T(8,128)S(1)} %fusion.45), channel_id=1, replica_groups=mesh['patch'=16,'col'=8] {'col'}, dimensions={0}, use_global_device_ids=true | all-gather | bytes 294912 | tf_op jit(solution)/shard_map/all_gather | solution.py:61
  565.0 61.8 %psum.107 = f32[16]{0:T(128)S(1)} all-reduce(f32[16]{0:T(128)S(1)} %get-tuple-element.69), channel_id=1, replica_groups=mesh['patch'=16,'col'=8] {'patch','col'}, use_global_device_ids=true, to_apply=%region_20.0 | all-reduce | flops 16 | bytes 128 | tf_op jit(solution)/shard_map/psum | solution.py:106
  627.0 63.5 %psum.108 = f32[16]{0:T(128)S(1)} all-reduce(f32[16]{0:T(128)S(1)} %multiply_reduce_fusion.3), channel_id=1, replica_groups=mesh['patch'=16,'col'=8] {'patch','col'}, use_global_device_ids=true, to_apply=%region_22.0 | all-reduce | flops 16 | bytes 128 | tf_op jit(solution)/shard_map/psum | solution.py:109
  695.8 14.1 %all_gather.26 = f32[32,16,128]{2,1,0:T(8,128)S(1)} all-gather(f32[4,16,128]{2,1,0:T(8,128)S(1)} %fusion.46), channel_id=1, replica_groups=mesh['patch'=16,'col'=8] {'col'}, dimensions={0}, use_global_device_ids=true | all-gather | bytes 294912 | tf_op jit(solution)/shard_map/all_gather | solution.py:61
  718.2 62.4 %psum.109 = f32[16]{0:T(128)S(1)} all-reduce(f32[16]{0:T(128)S(1)} %get-tuple-element.71), channel_id=1, replica_groups=mesh['patch'=16,'col'=8] {'patch','col'}, use_global_device_ids=true, to_apply=%region_24.0 | all-reduce | flops 16 | bytes 128 | tf_op jit(solution)/shard_map/psum | solution.py:106
  780.8 63.1 %psum.110 = f32[16]{0:T(128)S(1)} all-reduce(f32[16]{0:T(128)S(1)} %multiply_reduce_fusion.1), channel_id=1, replica_groups=mesh['patch'=16,'col'=8] {'patch','col'}, use_global_device_ids=true, to_apply=%region_26.0 | all-reduce | flops 16 | bytes 128 | tf_op jit(solution)/shard_map/psum | solution.py:106
  844.1 63.8 %psum.111 = f32[16]{0:T(128)S(1)} all-reduce(f32[16]{0:T(128)S(1)} %multiply_reduce_fusion), channel_id=1, replica_groups=mesh['patch'=16,'col'=8] {'patch','col'}, use_global_device_ids=true, to_apply=%region_28.0 | all-reduce | flops 16 | bytes 128 | tf_op jit(solution)/shard_map/psum | solution.py:109
  920.1 14.1 %all_gather.27 = f32[32,16,128]{2,1,0:T(8,128)S(1)} all-gather(f32[4,16,128]{2,1,0:T(8,128)S(1)} %add_add_fusion), channel_id=1, replica_groups=mesh['patch'=16,'col'=8] {'col'}, dimensions={0}, use_global_device_ids=true | all-gather | bytes 294912 | tf_op jit(solution)/shard_map/all_gather | solution.py:61
  934.9 8.0 fusion.3
  (125 shorter events, 90.2 us)
Async XLA Ops:
  0.6 73.7 %copy-start = (f32[4,128,128]{2,1,0:T(8,128)S(1)}, f32[4,128,128]{2,1,0:T(8,128)}, u32[]{:S(2)}) copy-start(f32[4,128,128]{2,1,0:T(8,128)} %param.28) | copy-start | bytes 786436
  0.6 103.7 %copy-start.1 = (f32[4,16,128]{2,1,0:T(8,128)S(1)}, f32[4,16,128]{2,1,0:T(8,128)}, u32[]{:S(2)}) copy-start(f32[4,16,128]{2,1,0:T(8,128)} %param.24) | copy-start | bytes 98308
  0.7 103.7 %copy-start.6 = (f32[4,128]{1,0:T(4,128)S(1)}, f32[4,128]{1,0:T(4,128)}, u32[]{:S(2)}) copy-start(f32[4,128]{1,0:T(4,128)} %param.26) | copy-start | bytes 6148
  0.7 103.7 %copy-start.5 = (f32[4,128]{1,0:T(4,128)S(1)}, f32[4,128]{1,0:T(4,128)}, u32[]{:S(2)}) copy-start(f32[4,128]{1,0:T(4,128)} %param.29) | copy-start | bytes 6148
  0.7 103.7 %copy-start.4 = (f32[4,128]{1,0:T(4,128)S(1)}, f32[4,128]{1,0:T(4,128)}, u32[]{:S(2)}) copy-start(f32[4,128]{1,0:T(4,128)} %param.30) | copy-start | bytes 6148
  0.7 23.3 %collective-permute-start = (f32[4,16,128]{2,1,0:T(8,128)}, f32[4,16,128]{2,1,0:T(8,128)S(1)}, u32[]{:S(2)}, u32[]{:S(2)}) collective-permute-start(f32[4,16,128]{2,1,0:T(8,128)} %param.24), channel_id=1, source_target_pairs={{0,8},{8,16},{16,24},{24,32},{32,40},{40,48},{48,56},{56,64},{64,7... | collective-permute-start | bytes 98312 | tf_op jit(solution)/shard_map/ppermute | solution.py:15
  2.8 21.2 %collective-permute-start.1 = (f32[4,16,128]{2,1,0:T(8,128)}, f32[4,16,128]{2,1,0:T(8,128)S(1)}, u32[]{:S(2)}, u32[]{:S(2)}) collective-permute-start(f32[4,16,128]{2,1,0:T(8,128)} %param.24), channel_id=1, source_target_pairs={{0,120},{8,0},{16,8},{24,16},{32,24},{40,32},{48,40},{56,48},{64,5... | collective-permute-start | bytes 98312 | tf_op jit(solution)/shard_map/ppermute | solution.py:15
  74.9 28.7 %collective-permute-start.2 = (f32[4,16,128]{2,1,0:T(8,128)S(1)}, f32[4,16,128]{2,1,0:T(8,128)S(1)}, u32[]{:S(2)}, u32[]{:S(2)}) collective-permute-start(f32[4,16,128]{2,1,0:T(8,128)S(1)} %fusion.43), channel_id=1, source_target_pairs={{0,8},{8,16},{16,24},{24,32},{32,40},{40,48},{48,56},{56,64},{64,7... | collective-permute-start | bytes 98312 | tf_op jit(solution)/shard_map/ppermute | solution.py:15
  74.9 28.6 %collective-permute-start.3 = (f32[4,16,128]{2,1,0:T(8,128)S(1)}, f32[4,16,128]{2,1,0:T(8,128)S(1)}, u32[]{:S(2)}, u32[]{:S(2)}) collective-permute-start(f32[4,16,128]{2,1,0:T(8,128)S(1)} %fusion.43), channel_id=1, source_target_pairs={{0,120},{8,0},{16,8},{24,16},{32,24},{40,32},{48,40},{56,48},{64,5... | collective-permute-start | bytes 98312 | tf_op jit(solution)/shard_map/ppermute | solution.py:15
  237.9 19.4 %collective-permute-start.4 = (f32[4,16,128]{2,1,0:T(8,128)S(1)}, f32[4,16,128]{2,1,0:T(8,128)S(1)}, u32[]{:S(2)}, u32[]{:S(2)}) collective-permute-start(f32[4,16,128]{2,1,0:T(8,128)S(1)} %fusion.44), channel_id=1, source_target_pairs={{0,8},{8,16},{16,24},{24,32},{32,40},{40,48},{48,56},{56,64},{64,7... | collective-permute-start | bytes 98312 | tf_op jit(solution)/shard_map/ppermute | solution.py:15
  238.0 19.3 %collective-permute-start.5 = (f32[4,16,128]{2,1,0:T(8,128)S(1)}, f32[4,16,128]{2,1,0:T(8,128)S(1)}, u32[]{:S(2)}, u32[]{:S(2)}) collective-permute-start(f32[4,16,128]{2,1,0:T(8,128)S(1)} %fusion.44), channel_id=1, source_target_pairs={{0,120},{8,0},{16,8},{24,16},{32,24},{40,32},{48,40},{56,48},{64,5... | collective-permute-start | bytes 98312 | tf_op jit(solution)/shard_map/ppermute | solution.py:15
  257.3 224.7 %copy-start.2 = (f32[4,16,128]{2,1,0:T(8,128)S(1)}, f32[4,16,128]{2,1,0:T(8,128)}, u32[]{:S(2)}) copy-start(f32[4,16,128]{2,1,0:T(8,128)} %param.25) | copy-start | bytes 98308
  462.3 18.9 %collective-permute-start.6 = (f32[4,16,128]{2,1,0:T(8,128)S(1)}, f32[4,16,128]{2,1,0:T(8,128)S(1)}, u32[]{:S(2)}, u32[]{:S(2)}) collective-permute-start(f32[4,16,128]{2,1,0:T(8,128)S(1)} %add_add_fusion.1), channel_id=1, source_target_pairs={{0,8},{8,16},{16,24},{24,32},{32,40},{40,48},{48,56},{56,64},{64,7... | collective-permute-start | bytes 98312 | tf_op jit(solution)/shard_map/ppermute | solution.py:15
  462.3 18.9 %collective-permute-start.7 = (f32[4,16,128]{2,1,0:T(8,128)S(1)}, f32[4,16,128]{2,1,0:T(8,128)S(1)}, u32[]{:S(2)}, u32[]{:S(2)}) collective-permute-start(f32[4,16,128]{2,1,0:T(8,128)S(1)} %add_add_fusion.1), channel_id=1, source_target_pairs={{0,120},{8,0},{16,8},{24,16},{32,24},{40,32},{48,40},{56,48},{64,5... | collective-permute-start | bytes 98312 | tf_op jit(solution)/shard_map/ppermute | solution.py:15
  530.5 26.3 %collective-permute-start.8 = (f32[4,16,128]{2,1,0:T(8,128)S(1)}, f32[4,16,128]{2,1,0:T(8,128)S(1)}, u32[]{:S(2)}, u32[]{:S(2)}) collective-permute-start(f32[4,16,128]{2,1,0:T(8,128)S(1)} %fusion.45), channel_id=1, source_target_pairs={{0,8},{8,16},{16,24},{24,32},{32,40},{40,48},{48,56},{56,64},{64,7... | collective-permute-start | bytes 98312 | tf_op jit(solution)/shard_map/ppermute | solution.py:15
  532.2 24.6 %collective-permute-start.9 = (f32[4,16,128]{2,1,0:T(8,128)S(1)}, f32[4,16,128]{2,1,0:T(8,128)S(1)}, u32[]{:S(2)}, u32[]{:S(2)}) collective-permute-start(f32[4,16,128]{2,1,0:T(8,128)S(1)} %fusion.45), channel_id=1, source_target_pairs={{0,120},{8,0},{16,8},{24,16},{32,24},{40,32},{48,40},{56,48},{64,5... | collective-permute-start | bytes 98312 | tf_op jit(solution)/shard_map/ppermute | solution.py:15
  691.0 19.0 %collective-permute-start.10 = (f32[4,16,128]{2,1,0:T(8,128)S(1)}, f32[4,16,128]{2,1,0:T(8,128)S(1)}, u32[]{:S(2)}, u32[]{:S(2)}) collective-permute-start(f32[4,16,128]{2,1,0:T(8,128)S(1)} %fusion.46), channel_id=1, source_target_pairs={{0,8},{8,16},{16,24},{24,32},{32,40},{40,48},{48,56},{56,64},{64,7... | collective-permute-start | bytes 98312 | tf_op jit(solution)/shard_map/ppermute | solution.py:15
  691.2 18.8 %collective-permute-start.11 = (f32[4,16,128]{2,1,0:T(8,128)S(1)}, f32[4,16,128]{2,1,0:T(8,128)S(1)}, u32[]{:S(2)}, u32[]{:S(2)}) collective-permute-start(f32[4,16,128]{2,1,0:T(8,128)S(1)} %fusion.46), channel_id=1, source_target_pairs={{0,120},{8,0},{16,8},{24,16},{32,24},{40,32},{48,40},{56,48},{64,5... | collective-permute-start | bytes 98312 | tf_op jit(solution)/shard_map/ppermute | solution.py:15
  915.2 27.7 %copy-start.3 = (f32[4,16,128]{2,1,0:T(8,128)}, f32[4,16,128]{2,1,0:T(8,128)S(1)}, u32[]{:S(2)}) copy-start(f32[4,16,128]{2,1,0:T(8,128)S(1)} %add_add_fusion) | copy-start | bytes 98308
  915.2 19.0 %collective-permute-start.12 = (f32[4,16,128]{2,1,0:T(8,128)S(1)}, f32[4,16,128]{2,1,0:T(8,128)S(1)}, u32[]{:S(2)}, u32[]{:S(2)}) collective-permute-start(f32[4,16,128]{2,1,0:T(8,128)S(1)} %add_add_fusion), channel_id=1, source_target_pairs={{0,8},{8,16},{16,24},{24,32},{32,40},{40,48},{48,56},{56,64},{64,7... | collective-permute-start | bytes 98312 | tf_op jit(solution)/shard_map/ppermute | solution.py:15
  915.3 18.9 %collective-permute-start.13 = (f32[4,16,128]{2,1,0:T(8,128)S(1)}, f32[4,16,128]{2,1,0:T(8,128)S(1)}, u32[]{:S(2)}, u32[]{:S(2)}) collective-permute-start(f32[4,16,128]{2,1,0:T(8,128)S(1)} %add_add_fusion), channel_id=1, source_target_pairs={{0,120},{8,0},{16,8},{24,16},{32,24},{40,32},{48,40},{56,48},{64,5... | collective-permute-start | bytes 98312 | tf_op jit(solution)/shard_map/ppermute | solution.py:15
